TPU v7x, 32 devices: a whole 2x2x4 slice. The times are simulated.
32 devices in a mesh: groups: 2 (over y), site: 4 (over z), sample: 4 (over x, core).
Axes of the slice: x: 2, y: 2, z: 4, core: 2. Of those that a mesh axis runs over, the one named last changes fastest.
Arguments:
- site_tensor: bfloat16 [8, 2048, 2, 2048], P(('groups', 'site'), None, None, 'sample'), parts along dimension 0, may hold values from -0.25 to 0.25
- fronts_in: bfloat16 [3072, 2048], P(('groups', 'sample')), parts along dimension 0
- outcomes: int32 [8, 1536], P(('groups', 'site'), 'sample'), parts along dimension 0, may hold values from 0 to 1
- charges: int32 [10, 16], P('groups'), parts along dimension 0, may hold values from 0 to 3
Outputs:
- fronts_out: bfloat16 [8, 1536, 2048], P(('groups', 'site'), 'sample'), parts along dimension 0
- log_steps: float32 [8, 1536], P(('groups', 'site'), 'sample'), parts along dimension 0
There are 2 independent parts, one for each index of `groups`. A program takes and returns all parts, laid end to end along the dimension named above; each array names one. Nothing has to cross between parts.
All inputs are finite; a program needn't handle non-finite values.
Results may differ from a plain program's by a relative error of at most 0.012.
Values may be sent and summed in bfloat16 or wider, within the bound.
No kernel may reach another device: no remote copies, remote signals or barrier semaphores. Data moves between devices by JAX's collectives and lax.ppermute only.
A program may use at most 128 MiB of HBM per device.

v0:
```python
import jax
import jax.numpy as jnp
from jax import lax
from jax.sharding import PartitionSpec as P

BLOCK = 128
CHARGES = 4
epsilon = 1e-06


def shifted(array, axis, by):
    count = lax.axis_size(axis)
    pairs = [(i, i + by) for i in range(count) if 0 <= i + by < count]
    return lax.ppermute(array, axis, pairs)


def block_mask(left_charge, right_charge):
    phases = jnp.arange(2, dtype=jnp.int32)
    return (
        right_charge[None, None, :]
        == (left_charge[:, None, None] + phases[None, :, None]) % CHARGES
    )


def per_device(site_tensor, fronts_in, outcomes, charges):
    owner_idx = lax.axis_index("site")
    site_count = lax.axis_size("site")
    left_charge = lax.dynamic_index_in_dim(charges, owner_idx, 0, keepdims=False)
    right_charge = lax.dynamic_index_in_dim(charges, owner_idx + 1, 0, keepdims=False)
    micro_count = 8
    sections = micro_count + site_count - 1
    row_count = fronts_in.shape[0]
    gathered = lax.all_gather(site_tensor, "sample", axis=3, tiled=True)[0]
    bond_width = gathered.shape[0]
    blocks = bond_width // BLOCK
    allowed = block_mask(left_charge, right_charge).astype(gathered.dtype)
    masked = (
        gathered.reshape(blocks, BLOCK, 2, blocks, BLOCK) * allowed[:, None, :, :, None]
    ).reshape(bond_width, 2 * bond_width)
    micro_rows = row_count // micro_count
    picks_all = outcomes[0]

    def advance(front_rows, picks):
        products = jnp.dot(front_rows, masked, preferred_element_type=jnp.float32).reshape(
            micro_rows, 2, bond_width
        )
        chosen = jnp.where(picks[:, None] == 1, products[:, 1], products[:, 0])
        row_norm = jnp.sqrt(jnp.mean(chosen * chosen, axis=1) + epsilon)
        return ((chosen / row_norm[:, None]).astype(jnp.bfloat16), jnp.log(row_norm))

    def skipped(front_rows, picks):
        return (front_rows, jnp.zeros((micro_rows,), jnp.float32))

    def section(section_idx, loop_state):
        received, out_fronts, out_logs = loop_state
        micro_idx = section_idx - owner_idx
        active = (micro_idx >= 0) & (micro_idx < micro_count)
        row_start = jnp.clip(micro_idx, 0, micro_count - 1) * micro_rows
        first_rows = lax.dynamic_slice_in_dim(fronts_in, row_start, micro_rows, 0)
        incoming = jnp.where(owner_idx == 0, first_rows, received)
        picks = lax.dynamic_slice_in_dim(picks_all, row_start, micro_rows, 0)
        new_front, log_norm = lax.cond(active, advance, skipped, incoming, picks)
        old_front = lax.dynamic_slice_in_dim(out_fronts, row_start, micro_rows, 0)
        old_logs = lax.dynamic_slice_in_dim(out_logs, row_start, micro_rows, 0)
        out_fronts = lax.dynamic_update_slice_in_dim(
            out_fronts, jnp.where(active, new_front, old_front), row_start, 0
        )
        out_logs = lax.dynamic_update_slice_in_dim(
            out_logs, jnp.where(active, log_norm, old_logs), row_start, 0
        )
        passed = shifted(new_front, "site", 1)
        return (passed, out_fronts, out_logs)

    initial = (
        jnp.zeros((micro_rows, bond_width), jnp.bfloat16),
        jnp.zeros((row_count, bond_width), jnp.bfloat16),
        jnp.zeros((row_count,), jnp.float32),
    )
    final_state = lax.fori_loop(0, sections, section, initial)
    return (final_state[1][None], final_state[2][None])


def solution(mesh):
    in_specs = (
        P(("groups", "site"), None, None, "sample"),
        P(("groups", "sample"), None),
        P(("groups", "site"), "sample"),
        P("groups", None),
    )
    out_specs = (P(("groups", "site"), "sample", None), P(("groups", "site"), "sample"))
    return jax.shard_map(
        per_device, mesh=mesh, in_specs=in_specs, out_specs=out_specs, check_vma=False
    )
```

profile of v0, /device:TPU:24, one launch (start us, length us, event | category | flops | bytes accessed | tf_op | source)
XLA Modules:
  0.0 360.7 jit_solution(17284264981978438301)
XLA Ops:
  15.0 26.2 %mul.23 = bf16[2048,4096]{1,0:T(8,128)(2,1)} reshape(bf16[16,128,2,16,128]{4,3,2,1,0:T(8,128)(2,1)} %mul.22) | data formatting | bytes 33554432 | tf_op jit(solution)/shard_map/mul | solution.py:38
  41.1 77.5 %all-gather.2.cloned.1.call-done = bf16[1,2048,2,2048]{3,2,1,0:T(2,128)(2,1)} async-done(((bf16[1,2048,2,512]{3,2,1,0:T(2,128)(2,1)}), bf16[1,2048,2,2048]{3,2,1,0:T(2,128)(2,1)}) %all-gather.2.cloned.1.call-update) | async-done | bytes 16777232 | tf_op jit(solution)/shard_map/all_gather | solution.py:33
  118.7 13.1 %copy.10 = bf16[256,8,2,2048]{3,1,2,0:T(8,128)(2,1)S(1)} copy(bf16[256,8,2,2048]{3,2,1,0:T(2,128)(2,1)} %bitcast.29) | data formatting | bytes 33554432
  131.8 9.3 %mul.24 = bf16[2048,4096]{1,0:T(8,128)(2,1)} multiply(bf16[2048,4096]{1,0:T(8,128)(2,1)S(1)} %bitcast.28, bf16[2048,4096]{1,0:T(8,128)(2,1)S(1)} %copy-done) | non-fusion elementwise | flops 8388608 | bytes 50331648 | tf_op jit(solution)/shard_map/mul | solution.py:38
  141.3 211.4 %while.18 = (s32[]{:T(128)}, bf16[48,2048]{1,0:T(8,128)(2,1)S(1)}, bf16[384,2048]{1,0:T(8,128)(2,1)S(1)}, f32[384]{0:T(512)S(1)}, s32[]{:T(128)}, /*index=5*/pre...) while((s32[]{:T(128)}, bf16[48,2048]{1,0:T(8,128)(2,1)S(1)}, ...), condition=%wide.region_4.5_spmd, body=%wide.region_0.4_spmd.sunk | while | flops 806092992 | bytes 24644720 | solution.py:79
  143.9 7.4 %collective-permute-done = bf16[48,2048]{1,0:T(8,128)(2,1)S(1)} collective-permute-done((bf16[48,2048]{1,0:T(8,128)(2,1)S(1)}, bf16[48,2048]{1,0:T(8,128)(2,1)S(1)}, u32[]{:S(2)}, u32[]{:S(2)}) %collective-permute-start) | collective-permute-done | bytes 196640 | tf_op jit(solution)/shard_map/while/body/eval_jaxpr/ppermute | solution.py:14
  153.9 6.6 %collective-permute-done = bf16[48,2048]{1,0:T(8,128)(2,1)S(1)} collective-permute-done((bf16[48,2048]{1,0:T(8,128)(2,1)S(1)}, bf16[48,2048]{1,0:T(8,128)(2,1)S(1)}, u32[]{:S(2)}, u32[]{:S(2)}) %collective-permute-start) | collective-permute-done | bytes 196640 | tf_op jit(solution)/shard_map/while/body/eval_jaxpr/ppermute | solution.py:14
  163.0 34.7 %collective-permute-done = bf16[48,2048]{1,0:T(8,128)(2,1)S(1)} collective-permute-done((bf16[48,2048]{1,0:T(8,128)(2,1)S(1)}, bf16[48,2048]{1,0:T(8,128)(2,1)S(1)}, u32[]{:S(2)}, u32[]{:S(2)}) %collective-permute-start) | collective-permute-done | bytes 196640 | tf_op jit(solution)/shard_map/while/body/eval_jaxpr/ppermute | solution.py:14
  198.7 10.8 %conditional.2 = (bf16[48,2048]{1,0:T(8,128)(2,1)S(1)}, f32[48]{0:T(128)S(1)}) conditional(s32[]{:T(128)} %convert_element_type.22, bf16[48,2048]{1,0:T(8,128)(2,1)S(1)} %dynamic-slice_select_fusion.2, (s32[384]{0:T(512)S(1)}, s32[]{:T(128)}, bf16[48,2048]{1,0:T(8,128)(2,1)S(1)}, bf16[2048,4096]{1,0:T(8,128)(2,1)}) %tuple.53), branch_computations={%region_1.1_spmd, %region_2.3_spmd} | conditional | flops 805896320 | bytes 22676772 | solution.py:62
  198.7 8.8 %fusion.8 = f32[48,4096]{1,0:T(8,128)S(1)} fusion(bf16[48,2048]{1,0:T(8,128)(2,1)S(1)} %get-tuple-element.177, bf16[2048,4096]{1,0:T(8,128)(2,1)} %get-tuple-element.178), kind=kOutput, calls=%fused_computation.24 | convolution fusion | flops 805306368 | bytes 17760256 | tf_op jit(solution)/shard_map/while/body/eval_jaxpr/cond/branch_1_fun/dot_general | solution.py:44
  218.1 10.8 %conditional.2 = (bf16[48,2048]{1,0:T(8,128)(2,1)S(1)}, f32[48]{0:T(128)S(1)}) conditional(s32[]{:T(128)} %convert_element_type.22, bf16[48,2048]{1,0:T(8,128)(2,1)S(1)} %dynamic-slice_select_fusion.2, (s32[384]{0:T(512)S(1)}, s32[]{:T(128)}, bf16[48,2048]{1,0:T(8,128)(2,1)S(1)}, bf16[2048,4096]{1,0:T(8,128)(2,1)}) %tuple.53), branch_computations={%region_1.1_spmd, %region_2.3_spmd} | conditional | flops 805896320 | bytes 22676772 | solution.py:62
  218.1 8.8 %fusion.8 = f32[48,4096]{1,0:T(8,128)S(1)} fusion(bf16[48,2048]{1,0:T(8,128)(2,1)S(1)} %get-tuple-element.177, bf16[2048,4096]{1,0:T(8,128)(2,1)} %get-tuple-element.178), kind=kOutput, calls=%fused_computation.24 | convolution fusion | flops 805306368 | bytes 17760256 | tf_op jit(solution)/shard_map/while/body/eval_jaxpr/cond/branch_1_fun/dot_general | solution.py:44
  237.5 10.8 %conditional.2 = (bf16[48,2048]{1,0:T(8,128)(2,1)S(1)}, f32[48]{0:T(128)S(1)}) conditional(s32[]{:T(128)} %convert_element_type.22, bf16[48,2048]{1,0:T(8,128)(2,1)S(1)} %dynamic-slice_select_fusion.2, (s32[384]{0:T(512)S(1)}, s32[]{:T(128)}, bf16[48,2048]{1,0:T(8,128)(2,1)S(1)}, bf16[2048,4096]{1,0:T(8,128)(2,1)}) %tuple.53), branch_computations={%region_1.1_spmd, %region_2.3_spmd} | conditional | flops 805896320 | bytes 22676772 | solution.py:62
  237.5 8.8 %fusion.8 = f32[48,4096]{1,0:T(8,128)S(1)} fusion(bf16[48,2048]{1,0:T(8,128)(2,1)S(1)} %get-tuple-element.177, bf16[2048,4096]{1,0:T(8,128)(2,1)} %get-tuple-element.178), kind=kOutput, calls=%fused_computation.24 | convolution fusion | flops 805306368 | bytes 17760256 | tf_op jit(solution)/shard_map/while/body/eval_jaxpr/cond/branch_1_fun/dot_general | solution.py:44
  256.8 10.8 %conditional.2 = (bf16[48,2048]{1,0:T(8,128)(2,1)S(1)}, f32[48]{0:T(128)S(1)}) conditional(s32[]{:T(128)} %convert_element_type.22, bf16[48,2048]{1,0:T(8,128)(2,1)S(1)} %dynamic-slice_select_fusion.2, (s32[384]{0:T(512)S(1)}, s32[]{:T(128)}, bf16[48,2048]{1,0:T(8,128)(2,1)S(1)}, bf16[2048,4096]{1,0:T(8,128)(2,1)}) %tuple.53), branch_computations={%region_1.1_spmd, %region_2.3_spmd} | conditional | flops 805896320 | bytes 22676772 | solution.py:62
  256.8 8.8 %fusion.8 = f32[48,4096]{1,0:T(8,128)S(1)} fusion(bf16[48,2048]{1,0:T(8,128)(2,1)S(1)} %get-tuple-element.177, bf16[2048,4096]{1,0:T(8,128)(2,1)} %get-tuple-element.178), kind=kOutput, calls=%fused_computation.24 | convolution fusion | flops 805306368 | bytes 17760256 | tf_op jit(solution)/shard_map/while/body/eval_jaxpr/cond/branch_1_fun/dot_general | solution.py:44
  276.2 10.8 %conditional.2 = (bf16[48,2048]{1,0:T(8,128)(2,1)S(1)}, f32[48]{0:T(128)S(1)}) conditional(s32[]{:T(128)} %convert_element_type.22, bf16[48,2048]{1,0:T(8,128)(2,1)S(1)} %dynamic-slice_select_fusion.2, (s32[384]{0:T(512)S(1)}, s32[]{:T(128)}, bf16[48,2048]{1,0:T(8,128)(2,1)S(1)}, bf16[2048,4096]{1,0:T(8,128)(2,1)}) %tuple.53), branch_computations={%region_1.1_spmd, %region_2.3_spmd} | conditional | flops 805896320 | bytes 22676772 | solution.py:62
  276.2 8.8 %fusion.8 = f32[48,4096]{1,0:T(8,128)S(1)} fusion(bf16[48,2048]{1,0:T(8,128)(2,1)S(1)} %get-tuple-element.177, bf16[2048,4096]{1,0:T(8,128)(2,1)} %get-tuple-element.178), kind=kOutput, calls=%fused_computation.24 | convolution fusion | flops 805306368 | bytes 17760256 | tf_op jit(solution)/shard_map/while/body/eval_jaxpr/cond/branch_1_fun/dot_general | solution.py:44
  295.6 10.8 %conditional.2 = (bf16[48,2048]{1,0:T(8,128)(2,1)S(1)}, f32[48]{0:T(128)S(1)}) conditional(s32[]{:T(128)} %convert_element_type.22, bf16[48,2048]{1,0:T(8,128)(2,1)S(1)} %dynamic-slice_select_fusion.2, (s32[384]{0:T(512)S(1)}, s32[]{:T(128)}, bf16[48,2048]{1,0:T(8,128)(2,1)S(1)}, bf16[2048,4096]{1,0:T(8,128)(2,1)}) %tuple.53), branch_computations={%region_1.1_spmd, %region_2.3_spmd} | conditional | flops 805896320 | bytes 22676772 | solution.py:62
  295.6 8.8 %fusion.8 = f32[48,4096]{1,0:T(8,128)S(1)} fusion(bf16[48,2048]{1,0:T(8,128)(2,1)S(1)} %get-tuple-element.177, bf16[2048,4096]{1,0:T(8,128)(2,1)} %get-tuple-element.178), kind=kOutput, calls=%fused_computation.24 | convolution fusion | flops 805306368 | bytes 17760256 | tf_op jit(solution)/shard_map/while/body/eval_jaxpr/cond/branch_1_fun/dot_general | solution.py:44
  315.0 10.8 %conditional.2 = (bf16[48,2048]{1,0:T(8,128)(2,1)S(1)}, f32[48]{0:T(128)S(1)}) conditional(s32[]{:T(128)} %convert_element_type.22, bf16[48,2048]{1,0:T(8,128)(2,1)S(1)} %dynamic-slice_select_fusion.2, (s32[384]{0:T(512)S(1)}, s32[]{:T(128)}, bf16[48,2048]{1,0:T(8,128)(2,1)S(1)}, bf16[2048,4096]{1,0:T(8,128)(2,1)}) %tuple.53), branch_computations={%region_1.1_spmd, %region_2.3_spmd} | conditional | flops 805896320 | bytes 22676772 | solution.py:62
  315.0 8.8 %fusion.8 = f32[48,4096]{1,0:T(8,128)S(1)} fusion(bf16[48,2048]{1,0:T(8,128)(2,1)S(1)} %get-tuple-element.177, bf16[2048,4096]{1,0:T(8,128)(2,1)} %get-tuple-element.178), kind=kOutput, calls=%fused_computation.24 | convolution fusion | flops 805306368 | bytes 17760256 | tf_op jit(solution)/shard_map/while/body/eval_jaxpr/cond/branch_1_fun/dot_general | solution.py:44
  334.3 10.8 %conditional.2 = (bf16[48,2048]{1,0:T(8,128)(2,1)S(1)}, f32[48]{0:T(128)S(1)}) conditional(s32[]{:T(128)} %convert_element_type.22, bf16[48,2048]{1,0:T(8,128)(2,1)S(1)} %dynamic-slice_select_fusion.2, (s32[384]{0:T(512)S(1)}, s32[]{:T(128)}, bf16[48,2048]{1,0:T(8,128)(2,1)S(1)}, bf16[2048,4096]{1,0:T(8,128)(2,1)}) %tuple.53), branch_computations={%region_1.1_spmd, %region_2.3_spmd} | conditional | flops 805896320 | bytes 22676772 | solution.py:62
  334.3 8.8 %fusion.8 = f32[48,4096]{1,0:T(8,128)S(1)} fusion(bf16[48,2048]{1,0:T(8,128)(2,1)S(1)} %get-tuple-element.177, bf16[2048,4096]{1,0:T(8,128)(2,1)} %get-tuple-element.178), kind=kOutput, calls=%fused_computation.24 | convolution fusion | flops 805306368 | bytes 17760256 | tf_op jit(solution)/shard_map/while/body/eval_jaxpr/cond/branch_1_fun/dot_general | solution.py:44
  (123 shorter events, 100.8 us)
Async XLA Ops:
  7.2 111.5 %all-gather.2.cloned.1.call-start = ((), (), s32[]{:S(2)}) async-start(), calls=%async_computation | async-start | bytes 20971520 | tf_op jit(solution)/shard_map/all_gather | solution.py:33
  14.9 26.2 %copy-start.2 = (s32[1,384]{1,0:T(1,128)S(1)}, s32[1,384]{1,0:T(1,128)}, u32[]{:S(2)}) copy-start(s32[1,384]{1,0:T(1,128)} %param.10) | copy-start | bytes 4612
  118.7 13.2 %copy-start = (bf16[2048,4096]{1,0:T(8,128)(2,1)S(1)}, bf16[2048,4096]{1,0:T(8,128)(2,1)}, u32[]{:S(2)}) copy-start(bf16[2048,4096]{1,0:T(8,128)(2,1)} %mul.23) | copy-start | bytes 50331652
  142.4 9.0 %collective-permute-start = (bf16[48,2048]{1,0:T(8,128)(2,1)S(1)}, bf16[48,2048]{1,0:T(8,128)(2,1)S(1)}, u32[]{:S(2)}, u32[]{:S(2)}) collective-permute-start(bf16[48,2048]{1,0:T(8,128)(2,1)S(1)} %get-tuple-element.278), channel_id=1, source_target_pairs={{0,4},{4,8},{8,12},{1,5},{5,9},{9,13},{2,6},{6,10},{10,14},{3,7},{... | collective-permute-start | bytes 589832 | tf_op jit(solution)/shard_map/while/body/eval_jaxpr/ppermute | solution.py:14
  152.4 8.1 %collective-permute-start = (bf16[48,2048]{1,0:T(8,128)(2,1)S(1)}, bf16[48,2048]{1,0:T(8,128)(2,1)S(1)}, u32[]{:S(2)}, u32[]{:S(2)}) collective-permute-start(bf16[48,2048]{1,0:T(8,128)(2,1)S(1)} %get-tuple-element.278), channel_id=1, source_target_pairs={{0,4},{4,8},{8,12},{1,5},{5,9},{9,13},{2,6},{6,10},{10,14},{3,7},{... | collective-permute-start | bytes 589832 | tf_op jit(solution)/shard_map/while/body/eval_jaxpr/ppermute | solution.py:14
  161.5 36.3 %collective-permute-start = (bf16[48,2048]{1,0:T(8,128)(2,1)S(1)}, bf16[48,2048]{1,0:T(8,128)(2,1)S(1)}, u32[]{:S(2)}, u32[]{:S(2)}) collective-permute-start(bf16[48,2048]{1,0:T(8,128)(2,1)S(1)} %get-tuple-element.278), channel_id=1, source_target_pairs={{0,4},{4,8},{8,12},{1,5},{5,9},{9,13},{2,6},{6,10},{10,14},{3,7},{... | collective-permute-start | bytes 589832 | tf_op jit(solution)/shard_map/while/body/eval_jaxpr/ppermute | solution.py:14
  209.5 7.6 %collective-permute-start = (bf16[48,2048]{1,0:T(8,128)(2,1)S(1)}, bf16[48,2048]{1,0:T(8,128)(2,1)S(1)}, u32[]{:S(2)}, u32[]{:S(2)}) collective-permute-start(bf16[48,2048]{1,0:T(8,128)(2,1)S(1)} %get-tuple-element.278), channel_id=1, source_target_pairs={{0,4},{4,8},{8,12},{1,5},{5,9},{9,13},{2,6},{6,10},{10,14},{3,7},{... | collective-permute-start | bytes 589832 | tf_op jit(solution)/shard_map/while/body/eval_jaxpr/ppermute | solution.py:14
  228.9 7.6 %collective-permute-start = (bf16[48,2048]{1,0:T(8,128)(2,1)S(1)}, bf16[48,2048]{1,0:T(8,128)(2,1)S(1)}, u32[]{:S(2)}, u32[]{:S(2)}) collective-permute-start(bf16[48,2048]{1,0:T(8,128)(2,1)S(1)} %get-tuple-element.278), channel_id=1, source_target_pairs={{0,4},{4,8},{8,12},{1,5},{5,9},{9,13},{2,6},{6,10},{10,14},{3,7},{... | collective-permute-start | bytes 589832 | tf_op jit(solution)/shard_map/while/body/eval_jaxpr/ppermute | solution.py:14
  248.3 7.6 %collective-permute-start = (bf16[48,2048]{1,0:T(8,128)(2,1)S(1)}, bf16[48,2048]{1,0:T(8,128)(2,1)S(1)}, u32[]{:S(2)}, u32[]{:S(2)}) collective-permute-start(bf16[48,2048]{1,0:T(8,128)(2,1)S(1)} %get-tuple-element.278), channel_id=1, source_target_pairs={{0,4},{4,8},{8,12},{1,5},{5,9},{9,13},{2,6},{6,10},{10,14},{3,7},{... | collective-permute-start | bytes 589832 | tf_op jit(solution)/shard_map/while/body/eval_jaxpr/ppermute | solution.py:14
  267.7 7.6 %collective-permute-start = (bf16[48,2048]{1,0:T(8,128)(2,1)S(1)}, bf16[48,2048]{1,0:T(8,128)(2,1)S(1)}, u32[]{:S(2)}, u32[]{:S(2)}) collective-permute-start(bf16[48,2048]{1,0:T(8,128)(2,1)S(1)} %get-tuple-element.278), channel_id=1, source_target_pairs={{0,4},{4,8},{8,12},{1,5},{5,9},{9,13},{2,6},{6,10},{10,14},{3,7},{... | collective-permute-start | bytes 589832 | tf_op jit(solution)/shard_map/while/body/eval_jaxpr/ppermute | solution.py:14
  287.0 7.6 %collective-permute-start = (bf16[48,2048]{1,0:T(8,128)(2,1)S(1)}, bf16[48,2048]{1,0:T(8,128)(2,1)S(1)}, u32[]{:S(2)}, u32[]{:S(2)}) collective-permute-start(bf16[48,2048]{1,0:T(8,128)(2,1)S(1)} %get-tuple-element.278), channel_id=1, source_target_pairs={{0,4},{4,8},{8,12},{1,5},{5,9},{9,13},{2,6},{6,10},{10,14},{3,7},{... | collective-permute-start | bytes 589832 | tf_op jit(solution)/shard_map/while/body/eval_jaxpr/ppermute | solution.py:14
  306.4 7.6 %collective-permute-start = (bf16[48,2048]{1,0:T(8,128)(2,1)S(1)}, bf16[48,2048]{1,0:T(8,128)(2,1)S(1)}, u32[]{:S(2)}, u32[]{:S(2)}) collective-permute-start(bf16[48,2048]{1,0:T(8,128)(2,1)S(1)} %get-tuple-element.278), channel_id=1, source_target_pairs={{0,4},{4,8},{8,12},{1,5},{5,9},{9,13},{2,6},{6,10},{10,14},{3,7},{... | collective-permute-start | bytes 589832 | tf_op jit(solution)/shard_map/while/body/eval_jaxpr/ppermute | solution.py:14
  325.8 7.6 %collective-permute-start = (bf16[48,2048]{1,0:T(8,128)(2,1)S(1)}, bf16[48,2048]{1,0:T(8,128)(2,1)S(1)}, u32[]{:S(2)}, u32[]{:S(2)}) collective-permute-start(bf16[48,2048]{1,0:T(8,128)(2,1)S(1)} %get-tuple-element.278), channel_id=1, source_target_pairs={{0,4},{4,8},{8,12},{1,5},{5,9},{9,13},{2,6},{6,10},{10,14},{3,7},{... | collective-permute-start | bytes 589832 | tf_op jit(solution)/shard_map/while/body/eval_jaxpr/ppermute | solution.py:14
  345.2 7.6 %collective-permute-start = (bf16[48,2048]{1,0:T(8,128)(2,1)S(1)}, bf16[48,2048]{1,0:T(8,128)(2,1)S(1)}, u32[]{:S(2)}, u32[]{:S(2)}) collective-permute-start(bf16[48,2048]{1,0:T(8,128)(2,1)S(1)} %get-tuple-element.278), channel_id=1, source_target_pairs={{0,4},{4,8},{8,12},{1,5},{5,9},{9,13},{2,6},{6,10},{10,14},{3,7},{... | collective-permute-start | bytes 589832 | tf_op jit(solution)/shard_map/while/body/eval_jaxpr/ppermute | solution.py:14
  352.7 1.1 copy-start.1
Sparse Core Ops, SparseCore 0:
  9.5 109.1 all-gather.1
where the time goes:
time: 362 us; the launch traced here: 361 us
  waiting for transfers between devices  175 us (48%)
  matrix products  70.3 us (19%)
  local copies, waits for them, and re-layouts  57.7 us (16%)
  other arithmetic  28.4 us (8%)
  starting transfers between devices  14.3 us (4%)
  between operations  14.1 us (4%)
    ppermute x11, waiting for transfers between devices, shifted(): return lax.ppermute(array, axis, pairs)  96.9 us
    all_gather x1, waiting for transfers between devices, per_device(): gathered = lax.all_gather(site_tensor, 'sample', axis=3, tiled=True)[0]  77.5 us
    dot_general x8, matrix products, advance(): jnp.dot(front_rows, masked, preferred_element_type=jnp.float32)  70.3 us
    mul x2, local copies, waits for them, and re-layouts, per_device(): gathered.reshape(blocks, BLOCK, 2, blocks, BLOCK)  32.2 us
    ppermute x11, starting transfers between devices, shifted(): return lax.ppermute(array, axis, pairs)  14.2 us
    unnamed x7, local copies, waits for them, and re-layouts  13.7 us
    select_n x11, other arithmetic, section(): incoming = jnp.where(owner_idx == 0, first_rows, received)  10.7 us
    mul x1, other arithmetic, per_device(): gathered.reshape(blocks, BLOCK, 2, blocks, BLOCK)  9.29 us
  transfers between devices with their start and end apart: 12, of which 12 were waited for; matrix products, arithmetic and copies ran while one was open for 10% of the time, Pallas kernels for 0%

commit v1 on v0

--- a/solution.py
+++ b/solution.py
@@ -6,6 +6,11 @@
 BLOCK = 128
 CHARGES = 4
 epsilon = 1e-06
+
+
+def stack_and_merge(shard, axis, dim):
+    pieces = lax.all_gather(shard, axis)
+    return jnp.concatenate(pieces, axis=dim)
 
 
 def shifted(array, axis, by):
@@ -30,7 +35,7 @@
     micro_count = 8
     sections = micro_count + site_count - 1
     row_count = fronts_in.shape[0]
-    gathered = lax.all_gather(site_tensor, "sample", axis=3, tiled=True)[0]
+    gathered = stack_and_merge(site_tensor, "sample", 3)[0]
     bond_width = gathered.shape[0]
     blocks = bond_width // BLOCK
     allowed = block_mask(left_charge, right_charge).astype(gathered.dtype)

time: 362 us -> 396 us (1.094)
  waiting for transfers between devices: 175 us -> 202 us
  local copies, waits for them, and re-layouts: 57.7 us -> 65.3 us
    mul x2 -> x1, local copies, waits for them, and re-layouts: 32.2 us -> 2.84 us  [per_device(): gathered.reshape(blocks, BLOCK, 2, blocks, BLOCK)]
    all_gather x1, waiting for transfers between devices: 77.5 us -> 105 us  [stack_and_merge(): pieces = lax.all_gather(shard, axis)]
    all_gather x0 -> x1, local copies, waits for them, and re-layouts: none -> 21.6 us  [stack_and_merge(): pieces = lax.all_gather(shard, axis)]
    while x0 -> x1, local copies, waits for them, and re-layouts: none -> 20.8 us  [per_device(): final_state = lax.fori_loop(0, sections, section, initial)]
    unnamed x7 -> x5, local copies, waits for them, and re-layouts: 13.7 us -> 8.27 us
  transfers between devices with their start and end apart: 12 -> 12, of which waited for: 12 -> 12; matrix products, arithmetic and copies ran while one was open for 10% -> 1% of each run, Pallas kernels for 0% -> 0%
where the time goes in v1:
time: 396 us; the launch traced here: 394 us
  waiting for transfers between devices  202 us (51%)
  matrix products  70.3 us (18%)
  local copies, waits for them, and re-layouts  65.3 us (16%)
  other arithmetic  26.5 us (7%)
  starting transfers between devices  14.3 us (4%)
  between operations  14.1 us (4%)
    all_gather x1, waiting for transfers between devices, stack_and_merge(): pieces = lax.all_gather(shard, axis)  105 us
    ppermute x11, waiting for transfers between devices, shifted(): return lax.ppermute(array, axis, pairs)  96.9 us
    dot_general x8, matrix products, advance(): jnp.dot(front_rows, masked, preferred_element_type=jnp.float32)  70.3 us
    all_gather x1, local copies, waits for them, and re-layouts, stack_and_merge(): pieces = lax.all_gather(shard, axis)  21.6 us
    while x1, local copies, waits for them, and re-layouts, per_device(): final_state = lax.fori_loop(0, sections, section, initial)  20.8 us
    ppermute x11, starting transfers between devices, shifted(): return lax.ppermute(array, axis, pairs)  14.2 us
    select_n x11, other arithmetic, section(): incoming = jnp.where(owner_idx == 0, first_rows, received)  10.7 us
    unnamed x5, local copies, waits for them, and re-layouts  8.27 us
  transfers between devices with their start and end apart: 12, of which 12 were waited for; matrix products, arithmetic and copies ran while one was open for 1% of the time, Pallas kernels for 0%

profile of v1, /device:TPU:24, one launch (start us, length us, event | category | flops | bytes accessed | tf_op | source)
XLA Modules:
  0.0 393.6 jit_solution(16896623931776280732)
XLA Ops:
  13.6 105.5 %all-gather.3.cloned.1.call-done = bf16[4,2048,2,512]{3,1,2,0:T(8,128)(2,1)} async-done(((bf16[1,2048,2,512]{3,1,2,0:T(8,128)(2,1)}), bf16[4,2048,2,512]{3,1,2,0:T(8,128)(2,1)}) %all-gather.3.cloned.1.call-update) | async-done | bytes 16777232 | tf_op jit(solution)/shard_map/all_gather | solution.py:12
  119.1 21.6 %copy.15 = bf16[4,2048,2,512]{1,3,0,2:T(8,128)(2,1)} copy(bf16[4,2048,2,512]{3,1,2,0:T(8,128)(2,1)} %all-gather.3.cloned.1.call-done) | data formatting | bytes 33554432 | tf_op jit(solution)/shard_map/all_gather | solution.py:12
  146.5 6.8 %bitcast_multiply_fusion = bf16[2048,4096]{0,1:T(8,128)(2,1)} fusion(bf16[512,8,16,128]{3,2,1,0:T(8,128)(2,1)S(1)} %bitcast.35, bf16[4,2048,2,512]{1,3,0,2:T(8,128)(2,1)S(1)} %copy-done), kind=kLoop, calls=%fused_computation.13 | loop fusion | flops 8388608 | bytes 50331648 | tf_op jit(solution)/shard_map/mul | solution.py:43
  153.2 20.8 %copy.16 = bf16[2048,4096]{1,0:T(8,128)(2,1)} copy(bf16[2048,4096]{0,1:T(8,128)(2,1)} %bitcast_multiply_fusion) | data formatting | bytes 33554432 | tf_op jit(solution)/shard_map/while | solution.py:84
  174.3 211.4 %while.18 = (s32[]{:T(128)}, bf16[48,2048]{1,0:T(8,128)(2,1)S(1)}, bf16[384,2048]{1,0:T(8,128)(2,1)S(1)}, f32[384]{0:T(512)S(1)}, s32[]{:T(128)}, /*index=5*/pre...) while((s32[]{:T(128)}, bf16[48,2048]{1,0:T(8,128)(2,1)S(1)}, ...), condition=%wide.region_4.5_spmd, body=%wide.region_0.4_spmd.sunk | while | flops 806092992 | bytes 24644720 | solution.py:84
  176.8 7.4 %collective-permute-done = bf16[48,2048]{1,0:T(8,128)(2,1)S(1)} collective-permute-done((bf16[48,2048]{1,0:T(8,128)(2,1)S(1)}, bf16[48,2048]{1,0:T(8,128)(2,1)S(1)}, u32[]{:S(2)}, u32[]{:S(2)}) %collective-permute-start) | collective-permute-done | bytes 196640 | tf_op jit(solution)/shard_map/while/body/eval_jaxpr/ppermute | solution.py:19
  186.8 6.6 %collective-permute-done = bf16[48,2048]{1,0:T(8,128)(2,1)S(1)} collective-permute-done((bf16[48,2048]{1,0:T(8,128)(2,1)S(1)}, bf16[48,2048]{1,0:T(8,128)(2,1)S(1)}, u32[]{:S(2)}, u32[]{:S(2)}) %collective-permute-start) | collective-permute-done | bytes 196640 | tf_op jit(solution)/shard_map/while/body/eval_jaxpr/ppermute | solution.py:19
  195.9 34.7 %collective-permute-done = bf16[48,2048]{1,0:T(8,128)(2,1)S(1)} collective-permute-done((bf16[48,2048]{1,0:T(8,128)(2,1)S(1)}, bf16[48,2048]{1,0:T(8,128)(2,1)S(1)}, u32[]{:S(2)}, u32[]{:S(2)}) %collective-permute-start) | collective-permute-done | bytes 196640 | tf_op jit(solution)/shard_map/while/body/eval_jaxpr/ppermute | solution.py:19
  231.6 10.8 %conditional.2 = (bf16[48,2048]{1,0:T(8,128)(2,1)S(1)}, f32[48]{0:T(128)S(1)}) conditional(s32[]{:T(128)} %convert_element_type.22, bf16[48,2048]{1,0:T(8,128)(2,1)S(1)} %dynamic-slice_select_fusion.2, (s32[384]{0:T(512)S(1)}, s32[]{:T(128)}, bf16[48,2048]{1,0:T(8,128)(2,1)S(1)}, bf16[2048,4096]{1,0:T(8,128)(2,1)}) %tuple.54), branch_computations={%region_1.1_spmd, %region_2.3_spmd} | conditional | flops 805896320 | bytes 22676772 | solution.py:67
  231.6 8.8 %fusion.5 = f32[48,4096]{1,0:T(8,128)S(1)} fusion(bf16[48,2048]{1,0:T(8,128)(2,1)S(1)} %get-tuple-element.177, bf16[2048,4096]{1,0:T(8,128)(2,1)} %get-tuple-element.178), kind=kOutput, calls=%fused_computation.22 | convolution fusion | flops 805306368 | bytes 17760256 | tf_op jit(solution)/shard_map/while/body/eval_jaxpr/cond/branch_1_fun/dot_general | solution.py:49
  251.0 10.8 %conditional.2 = (bf16[48,2048]{1,0:T(8,128)(2,1)S(1)}, f32[48]{0:T(128)S(1)}) conditional(s32[]{:T(128)} %convert_element_type.22, bf16[48,2048]{1,0:T(8,128)(2,1)S(1)} %dynamic-slice_select_fusion.2, (s32[384]{0:T(512)S(1)}, s32[]{:T(128)}, bf16[48,2048]{1,0:T(8,128)(2,1)S(1)}, bf16[2048,4096]{1,0:T(8,128)(2,1)}) %tuple.54), branch_computations={%region_1.1_spmd, %region_2.3_spmd} | conditional | flops 805896320 | bytes 22676772 | solution.py:67
  251.0 8.8 %fusion.5 = f32[48,4096]{1,0:T(8,128)S(1)} fusion(bf16[48,2048]{1,0:T(8,128)(2,1)S(1)} %get-tuple-element.177, bf16[2048,4096]{1,0:T(8,128)(2,1)} %get-tuple-element.178), kind=kOutput, calls=%fused_computation.22 | convolution fusion | flops 805306368 | bytes 17760256 | tf_op jit(solution)/shard_map/while/body/eval_jaxpr/cond/branch_1_fun/dot_general | solution.py:49
  270.4 10.8 %conditional.2 = (bf16[48,2048]{1,0:T(8,128)(2,1)S(1)}, f32[48]{0:T(128)S(1)}) conditional(s32[]{:T(128)} %convert_element_type.22, bf16[48,2048]{1,0:T(8,128)(2,1)S(1)} %dynamic-slice_select_fusion.2, (s32[384]{0:T(512)S(1)}, s32[]{:T(128)}, bf16[48,2048]{1,0:T(8,128)(2,1)S(1)}, bf16[2048,4096]{1,0:T(8,128)(2,1)}) %tuple.54), branch_computations={%region_1.1_spmd, %region_2.3_spmd} | conditional | flops 805896320 | bytes 22676772 | solution.py:67
  270.4 8.8 %fusion.5 = f32[48,4096]{1,0:T(8,128)S(1)} fusion(bf16[48,2048]{1,0:T(8,128)(2,1)S(1)} %get-tuple-element.177, bf16[2048,4096]{1,0:T(8,128)(2,1)} %get-tuple-element.178), kind=kOutput, calls=%fused_computation.22 | convolution fusion | flops 805306368 | bytes 17760256 | tf_op jit(solution)/shard_map/while/body/eval_jaxpr/cond/branch_1_fun/dot_general | solution.py:49
  289.8 10.8 %conditional.2 = (bf16[48,2048]{1,0:T(8,128)(2,1)S(1)}, f32[48]{0:T(128)S(1)}) conditional(s32[]{:T(128)} %convert_element_type.22, bf16[48,2048]{1,0:T(8,128)(2,1)S(1)} %dynamic-slice_select_fusion.2, (s32[384]{0:T(512)S(1)}, s32[]{:T(128)}, bf16[48,2048]{1,0:T(8,128)(2,1)S(1)}, bf16[2048,4096]{1,0:T(8,128)(2,1)}) %tuple.54), branch_computations={%region_1.1_spmd, %region_2.3_spmd} | conditional | flops 805896320 | bytes 22676772 | solution.py:67
  289.8 8.8 %fusion.5 = f32[48,4096]{1,0:T(8,128)S(1)} fusion(bf16[48,2048]{1,0:T(8,128)(2,1)S(1)} %get-tuple-element.177, bf16[2048,4096]{1,0:T(8,128)(2,1)} %get-tuple-element.178), kind=kOutput, calls=%fused_computation.22 | convolution fusion | flops 805306368 | bytes 17760256 | tf_op jit(solution)/shard_map/while/body/eval_jaxpr/cond/branch_1_fun/dot_general | solution.py:49
  309.1 10.8 %conditional.2 = (bf16[48,2048]{1,0:T(8,128)(2,1)S(1)}, f32[48]{0:T(128)S(1)}) conditional(s32[]{:T(128)} %convert_element_type.22, bf16[48,2048]{1,0:T(8,128)(2,1)S(1)} %dynamic-slice_select_fusion.2, (s32[384]{0:T(512)S(1)}, s32[]{:T(128)}, bf16[48,2048]{1,0:T(8,128)(2,1)S(1)}, bf16[2048,4096]{1,0:T(8,128)(2,1)}) %tuple.54), branch_computations={%region_1.1_spmd, %region_2.3_spmd} | conditional | flops 805896320 | bytes 22676772 | solution.py:67
  309.1 8.8 %fusion.5 = f32[48,4096]{1,0:T(8,128)S(1)} fusion(bf16[48,2048]{1,0:T(8,128)(2,1)S(1)} %get-tuple-element.177, bf16[2048,4096]{1,0:T(8,128)(2,1)} %get-tuple-element.178), kind=kOutput, calls=%fused_computation.22 | convolution fusion | flops 805306368 | bytes 17760256 | tf_op jit(solution)/shard_map/while/body/eval_jaxpr/cond/branch_1_fun/dot_general | solution.py:49
  328.5 10.8 %conditional.2 = (bf16[48,2048]{1,0:T(8,128)(2,1)S(1)}, f32[48]{0:T(128)S(1)}) conditional(s32[]{:T(128)} %convert_element_type.22, bf16[48,2048]{1,0:T(8,128)(2,1)S(1)} %dynamic-slice_select_fusion.2, (s32[384]{0:T(512)S(1)}, s32[]{:T(128)}, bf16[48,2048]{1,0:T(8,128)(2,1)S(1)}, bf16[2048,4096]{1,0:T(8,128)(2,1)}) %tuple.54), branch_computations={%region_1.1_spmd, %region_2.3_spmd} | conditional | flops 805896320 | bytes 22676772 | solution.py:67
  328.5 8.8 %fusion.5 = f32[48,4096]{1,0:T(8,128)S(1)} fusion(bf16[48,2048]{1,0:T(8,128)(2,1)S(1)} %get-tuple-element.177, bf16[2048,4096]{1,0:T(8,128)(2,1)} %get-tuple-element.178), kind=kOutput, calls=%fused_computation.22 | convolution fusion | flops 805306368 | bytes 17760256 | tf_op jit(solution)/shard_map/while/body/eval_jaxpr/cond/branch_1_fun/dot_general | solution.py:49
  347.9 10.8 %conditional.2 = (bf16[48,2048]{1,0:T(8,128)(2,1)S(1)}, f32[48]{0:T(128)S(1)}) conditional(s32[]{:T(128)} %convert_element_type.22, bf16[48,2048]{1,0:T(8,128)(2,1)S(1)} %dynamic-slice_select_fusion.2, (s32[384]{0:T(512)S(1)}, s32[]{:T(128)}, bf16[48,2048]{1,0:T(8,128)(2,1)S(1)}, bf16[2048,4096]{1,0:T(8,128)(2,1)}) %tuple.54), branch_computations={%region_1.1_spmd, %region_2.3_spmd} | conditional | flops 805896320 | bytes 22676772 | solution.py:67
  347.9 8.8 %fusion.5 = f32[48,4096]{1,0:T(8,128)S(1)} fusion(bf16[48,2048]{1,0:T(8,128)(2,1)S(1)} %get-tuple-element.177, bf16[2048,4096]{1,0:T(8,128)(2,1)} %get-tuple-element.178), kind=kOutput, calls=%fused_computation.22 | convolution fusion | flops 805306368 | bytes 17760256 | tf_op jit(solution)/shard_map/while/body/eval_jaxpr/cond/branch_1_fun/dot_general | solution.py:49
  367.2 10.8 %conditional.2 = (bf16[48,2048]{1,0:T(8,128)(2,1)S(1)}, f32[48]{0:T(128)S(1)}) conditional(s32[]{:T(128)} %convert_element_type.22, bf16[48,2048]{1,0:T(8,128)(2,1)S(1)} %dynamic-slice_select_fusion.2, (s32[384]{0:T(512)S(1)}, s32[]{:T(128)}, bf16[48,2048]{1,0:T(8,128)(2,1)S(1)}, bf16[2048,4096]{1,0:T(8,128)(2,1)}) %tuple.54), branch_computations={%region_1.1_spmd, %region_2.3_spmd} | conditional | flops 805896320 | bytes 22676772 | solution.py:67
  367.3 8.8 %fusion.5 = f32[48,4096]{1,0:T(8,128)S(1)} fusion(bf16[48,2048]{1,0:T(8,128)(2,1)S(1)} %get-tuple-element.177, bf16[2048,4096]{1,0:T(8,128)(2,1)} %get-tuple-element.178), kind=kOutput, calls=%fused_computation.22 | convolution fusion | flops 805306368 | bytes 17760256 | tf_op jit(solution)/shard_map/while/body/eval_jaxpr/cond/branch_1_fun/dot_general | solution.py:49
  (122 shorter events, 105.2 us)
Async XLA Ops:
  7.2 111.9 %all-gather.3.cloned.1.call-start = ((), (), s32[]{:S(2)}) async-start(), calls=%async_computation | async-start | bytes 20971520 | tf_op jit(solution)/shard_map/all_gather | solution.py:12
  140.7 5.8 %copy-start = (bf16[4,2048,2,512]{1,3,0,2:T(8,128)(2,1)S(1)}, bf16[4,2048,2,512]{1,3,0,2:T(8,128)(2,1)}, u32[]{:S(2)}) copy-start(bf16[4,2048,2,512]{1,3,0,2:T(8,128)(2,1)} %copy.15) | copy-start | bytes 50331652
  175.3 9.0 %collective-permute-start = (bf16[48,2048]{1,0:T(8,128)(2,1)S(1)}, bf16[48,2048]{1,0:T(8,128)(2,1)S(1)}, u32[]{:S(2)}, u32[]{:S(2)}) collective-permute-start(bf16[48,2048]{1,0:T(8,128)(2,1)S(1)} %get-tuple-element.287), channel_id=1, source_target_pairs={{0,4},{4,8},{8,12},{1,5},{5,9},{9,13},{2,6},{6,10},{10,14},{3,7},{... | collective-permute-start | bytes 589832 | tf_op jit(solution)/shard_map/while/body/eval_jaxpr/ppermute | solution.py:19
  185.3 8.1 %collective-permute-start = (bf16[48,2048]{1,0:T(8,128)(2,1)S(1)}, bf16[48,2048]{1,0:T(8,128)(2,1)S(1)}, u32[]{:S(2)}, u32[]{:S(2)}) collective-permute-start(bf16[48,2048]{1,0:T(8,128)(2,1)S(1)} %get-tuple-element.287), channel_id=1, source_target_pairs={{0,4},{4,8},{8,12},{1,5},{5,9},{9,13},{2,6},{6,10},{10,14},{3,7},{... | collective-permute-start | bytes 589832 | tf_op jit(solution)/shard_map/while/body/eval_jaxpr/ppermute | solution.py:19
  194.4 36.3 %collective-permute-start = (bf16[48,2048]{1,0:T(8,128)(2,1)S(1)}, bf16[48,2048]{1,0:T(8,128)(2,1)S(1)}, u32[]{:S(2)}, u32[]{:S(2)}) collective-permute-start(bf16[48,2048]{1,0:T(8,128)(2,1)S(1)} %get-tuple-element.287), channel_id=1, source_target_pairs={{0,4},{4,8},{8,12},{1,5},{5,9},{9,13},{2,6},{6,10},{10,14},{3,7},{... | collective-permute-start | bytes 589832 | tf_op jit(solution)/shard_map/while/body/eval_jaxpr/ppermute | solution.py:19
  242.5 7.6 %collective-permute-start = (bf16[48,2048]{1,0:T(8,128)(2,1)S(1)}, bf16[48,2048]{1,0:T(8,128)(2,1)S(1)}, u32[]{:S(2)}, u32[]{:S(2)}) collective-permute-start(bf16[48,2048]{1,0:T(8,128)(2,1)S(1)} %get-tuple-element.287), channel_id=1, source_target_pairs={{0,4},{4,8},{8,12},{1,5},{5,9},{9,13},{2,6},{6,10},{10,14},{3,7},{... | collective-permute-start | bytes 589832 | tf_op jit(solution)/shard_map/while/body/eval_jaxpr/ppermute | solution.py:19
  261.8 7.6 %collective-permute-start = (bf16[48,2048]{1,0:T(8,128)(2,1)S(1)}, bf16[48,2048]{1,0:T(8,128)(2,1)S(1)}, u32[]{:S(2)}, u32[]{:S(2)}) collective-permute-start(bf16[48,2048]{1,0:T(8,128)(2,1)S(1)} %get-tuple-element.287), channel_id=1, source_target_pairs={{0,4},{4,8},{8,12},{1,5},{5,9},{9,13},{2,6},{6,10},{10,14},{3,7},{... | collective-permute-start | bytes 589832 | tf_op jit(solution)/shard_map/while/body/eval_jaxpr/ppermute | solution.py:19
  281.2 7.6 %collective-permute-start = (bf16[48,2048]{1,0:T(8,128)(2,1)S(1)}, bf16[48,2048]{1,0:T(8,128)(2,1)S(1)}, u32[]{:S(2)}, u32[]{:S(2)}) collective-permute-start(bf16[48,2048]{1,0:T(8,128)(2,1)S(1)} %get-tuple-element.287), channel_id=1, source_target_pairs={{0,4},{4,8},{8,12},{1,5},{5,9},{9,13},{2,6},{6,10},{10,14},{3,7},{... | collective-permute-start | bytes 589832 | tf_op jit(solution)/shard_map/while/body/eval_jaxpr/ppermute | solution.py:19
  300.6 7.6 %collective-permute-start = (bf16[48,2048]{1,0:T(8,128)(2,1)S(1)}, bf16[48,2048]{1,0:T(8,128)(2,1)S(1)}, u32[]{:S(2)}, u32[]{:S(2)}) collective-permute-start(bf16[48,2048]{1,0:T(8,128)(2,1)S(1)} %get-tuple-element.287), channel_id=1, source_target_pairs={{0,4},{4,8},{8,12},{1,5},{5,9},{9,13},{2,6},{6,10},{10,14},{3,7},{... | collective-permute-start | bytes 589832 | tf_op jit(solution)/shard_map/while/body/eval_jaxpr/ppermute | solution.py:19
  320.0 7.6 %collective-permute-start = (bf16[48,2048]{1,0:T(8,128)(2,1)S(1)}, bf16[48,2048]{1,0:T(8,128)(2,1)S(1)}, u32[]{:S(2)}, u32[]{:S(2)}) collective-permute-start(bf16[48,2048]{1,0:T(8,128)(2,1)S(1)} %get-tuple-element.287), channel_id=1, source_target_pairs={{0,4},{4,8},{8,12},{1,5},{5,9},{9,13},{2,6},{6,10},{10,14},{3,7},{... | collective-permute-start | bytes 589832 | tf_op jit(solution)/shard_map/while/body/eval_jaxpr/ppermute | solution.py:19
  339.3 7.6 %collective-permute-start = (bf16[48,2048]{1,0:T(8,128)(2,1)S(1)}, bf16[48,2048]{1,0:T(8,128)(2,1)S(1)}, u32[]{:S(2)}, u32[]{:S(2)}) collective-permute-start(bf16[48,2048]{1,0:T(8,128)(2,1)S(1)} %get-tuple-element.287), channel_id=1, source_target_pairs={{0,4},{4,8},{8,12},{1,5},{5,9},{9,13},{2,6},{6,10},{10,14},{3,7},{... | collective-permute-start | bytes 589832 | tf_op jit(solution)/shard_map/while/body/eval_jaxpr/ppermute | solution.py:19
  358.7 7.6 %collective-permute-start = (bf16[48,2048]{1,0:T(8,128)(2,1)S(1)}, bf16[48,2048]{1,0:T(8,128)(2,1)S(1)}, u32[]{:S(2)}, u32[]{:S(2)}) collective-permute-start(bf16[48,2048]{1,0:T(8,128)(2,1)S(1)} %get-tuple-element.287), channel_id=1, source_target_pairs={{0,4},{4,8},{8,12},{1,5},{5,9},{9,13},{2,6},{6,10},{10,14},{3,7},{... | collective-permute-start | bytes 589832 | tf_op jit(solution)/shard_map/while/body/eval_jaxpr/ppermute | solution.py:19
  378.1 7.6 %collective-permute-start = (bf16[48,2048]{1,0:T(8,128)(2,1)S(1)}, bf16[48,2048]{1,0:T(8,128)(2,1)S(1)}, u32[]{:S(2)}, u32[]{:S(2)}) collective-permute-start(bf16[48,2048]{1,0:T(8,128)(2,1)S(1)} %get-tuple-element.287), channel_id=1, source_target_pairs={{0,4},{4,8},{8,12},{1,5},{5,9},{9,13},{2,6},{6,10},{10,14},{3,7},{... | collective-permute-start | bytes 589832 | tf_op jit(solution)/shard_map/while/body/eval_jaxpr/ppermute | solution.py:19
  385.6 1.1 copy-start.1
Sparse Core Ops, SparseCore 0:
  12.2 106.8 all-gather.2
